TPU v7x, 256 devices: a whole 4x4x8 slice. The times are simulated.
256 devices in a mesh: leaf: 64 (over x, z, core), front: 4 (over y).
Axes of the slice: x: 4, y: 4, z: 8, core: 2. Of those that a mesh axis runs over, the one named last changes fastest.
Arguments:
- child_update: bfloat16 [64, 4, 1, 3, 256, 3072], P('leaf', 'front'), may hold values from -60 to 60, as said below
- sep_one: bfloat16 [64, 4, 1, 4, 256, 512], P('leaf', 'front'), may hold values from -60 to 60, as said below
- sep_two: bfloat16 [64, 4, 1, 4, 256, 256], P('leaf', 'front'), may hold values from -60 to 60, as said below
- map_one: int32 [64, 1, 4, 3], replicated, may hold values from 0 to 3, as said below
- map_two: int32 [32, 1, 4, 3], replicated, may hold values from 0 to 3, as said below
- mask_one: int32 [32, 1, 12, 4], replicated, may hold values 0 or 1
- mask_two: int32 [16, 1, 12, 4], replicated, may hold values 0 or 1
Outputs:
- factor_one: float32 [64, 4, 1, 4, 256, 512], P('leaf', 'front')
- factor_two: float32 [64, 4, 1, 4, 256, 256], P('leaf', 'front')
- update_two: bfloat16 [64, 4, 1, 3, 256, 768], P('leaf', 'front')
Inputs may be any that keep to these rules, and one draw needn't show every extreme that they name: `child_update`: every child[l,b] is symmetric positive definite. `sep_one`: the top 1024 rows of each front's initial entries form a symmetric positive definite block, and every assembled front is positive definite. `sep_two`: the top 1024 rows of each front's initial entries form a symmetric positive definite block, and every assembled front is positive definite. `map_one`: for each child, batch and j the 3 entries are distinct; the two children 2p and 2p + 1 leave out different slots, so every parent tile receives one or two child tiles. `map_two`: for each first-level front, batch and j the 3 entries are distinct; fronts 2q and 2q + 1 leave out different slots, so every parent tile receives one or two child tiles.
All inputs are finite; a program needn't handle non-finite values.
Results may differ from a plain program's by a relative error of at most 0.0047.
Values may be sent and summed in bfloat16 or wider, within the bound.
A program may use at most 192 MiB of HBM per device.

v0:
```python
import jax
import jax.numpy as jnp
from jax import lax
from jax.sharding import PartitionSpec as P

TILE = 256
ST = 4
UT = 12
FT = 16
S = 1024
U = 3072
F = 4096


def swapped(value, axis, apart):
    mask = 2**apart
    pairs = [(source, source ^ mask) for source in range(lax.axis_size(axis))]
    return lax.ppermute(value, axis, pairs)


def place_tiles(blocks, row_source, row_live, col_source, col_live):
    taken = jnp.take(blocks, row_source, axis=0)
    taken = jnp.take(taken, col_source, axis=2)
    keep = jnp.logical_and(row_live[:, None, None, None], col_live[None, None, :, None])
    return jnp.where(keep, taken.astype(jnp.float32), 0.0)


def place_child(child_rows, tile_map, column):
    batch_count = child_rows.shape[0]
    local_tiles = child_rows.shape[1]
    groups = tile_map.shape[1]
    slot_count = FT // groups
    own_slots = lax.dynamic_index_in_dim(tile_map, column, 1, keepdims=False)
    row_hit = own_slots[..., None] == jnp.arange(slot_count, dtype=jnp.int32)
    row_source = jnp.sum(
        row_hit.astype(jnp.int32) * jnp.arange(local_tiles, dtype=jnp.int32)[None, :, None], axis=1
    )
    row_live = jnp.any(row_hit, axis=1)
    targets = (jnp.swapaxes(tile_map, 1, 2) * groups + jnp.arange(groups, dtype=jnp.int32)).reshape(
        batch_count, UT
    )
    col_hit = targets[..., None] == jnp.arange(FT, dtype=jnp.int32)
    col_source = jnp.sum(
        col_hit.astype(jnp.int32) * jnp.arange(UT, dtype=jnp.int32)[None, :, None], axis=1
    )
    col_live = jnp.any(col_hit, axis=1)
    blocks = child_rows.reshape(batch_count, local_tiles, TILE, UT, TILE)
    placed = jax.vmap(place_tiles)(blocks, row_source, row_live, col_source, col_live)
    return placed.reshape(batch_count, slot_count, TILE, F)


def join_halves(mine, other, position):
    lower_first = jnp.concatenate([mine, other], axis=-1)
    upper_first = jnp.concatenate([other, mine], axis=-1)
    return jnp.where(position == 0, lower_first, upper_first)


def add_initial(canvas, initial, mask_front, column):
    batch_count = canvas.shape[0]
    slot_count = canvas.shape[1]
    groups = lax.axis_size("front")
    mask_rows = mask_front.reshape(batch_count, slot_count - 1, groups, ST)
    mask_rows = lax.dynamic_index_in_dim(mask_rows, column, 2, keepdims=False).astype(jnp.float32)
    mask_all = jnp.concatenate([jnp.ones((batch_count, 1, ST), jnp.float32), mask_rows], axis=1)
    weighted = initial.astype(jnp.float32).reshape(batch_count, slot_count, TILE, ST, TILE)
    weighted = (weighted * mask_all[:, :, None, :, None]).reshape(batch_count, slot_count, TILE, S)
    return jnp.concatenate([canvas[:, :, :, :S] + weighted, canvas[:, :, :, S:]], axis=-1)


def factor_front(canvas, column):
    batch_count = canvas.shape[0]
    local_tiles = canvas.shape[1] - 1
    groups = lax.axis_size("front")
    pivot_piece = canvas[:, :1, :, :S]
    pivot_all = lax.all_gather(pivot_piece[None], "front", axis=0, tiled=True)
    pivot_block = jnp.moveaxis(pivot_all, 0, 2).reshape(batch_count, S, S)
    lower_factor = jnp.linalg.cholesky(pivot_block)
    coupling = canvas[:, 1:, :, :S].reshape(batch_count, local_tiles * TILE, S)
    panel_full = lax.linalg.triangular_solve(
        lower_factor, coupling, left_side=False, lower=True, transpose_a=True
    )
    panel_round = panel_full.astype(jnp.bfloat16)
    shared = lax.all_gather(
        panel_round.reshape(batch_count, local_tiles, TILE, S)[None], "front", axis=0, tiled=True
    )
    ordered = jnp.transpose(shared, (1, 2, 0, 3, 4)).reshape(batch_count, U, S)
    own_lower = lax.dynamic_index_in_dim(
        lower_factor.reshape(batch_count, groups, TILE, S), column, 1, keepdims=True
    )
    factor_rows = jnp.concatenate(
        [own_lower, panel_full.reshape(batch_count, local_tiles, TILE, S)], axis=1
    )
    trailing = canvas[:, 1:, :, S:].reshape(batch_count, local_tiles * TILE, U)
    product = jnp.einsum("brk,bnk->brn", panel_round, ordered, preferred_element_type=jnp.float32)
    update = (trailing - product).astype(jnp.bfloat16)
    return (factor_rows, update)


def body(child_update, sep_one, sep_two, map_one, map_two, mask_one, mask_two):
    column = lax.axis_index("front")
    leaf_index = lax.axis_index("leaf")
    half_index = leaf_index % 2
    quarter_index = leaf_index % 4
    pair_index = leaf_index // 2
    quad_index = leaf_index // 4
    side_index = pair_index % 2
    child_rows = child_update[0, 0]
    batch_count = child_rows.shape[0]
    local_tiles = child_rows.shape[1]
    entries_one = sep_one[0, 0]
    entries_two = sep_two[0, 0]
    peer_rows, peer_one, peer_two = swapped((child_rows, entries_one, entries_two), "leaf", 0)
    map_own = lax.dynamic_index_in_dim(map_one, leaf_index, 0, keepdims=False)
    map_peer = lax.dynamic_index_in_dim(map_one, jnp.bitwise_xor(leaf_index, 1), 0, keepdims=False)
    front_first = place_child(child_rows, map_own, column) + place_child(
        peer_rows, map_peer, column
    )
    initial_one = join_halves(entries_one, peer_one, half_index)
    mask_front = lax.dynamic_index_in_dim(mask_one, pair_index, 0, keepdims=False)
    front_first = add_initial(front_first, initial_one, mask_front, column)
    factor_rows_one, update_one = factor_front(front_first, column)
    factor_one = lax.dynamic_slice_in_dim(factor_rows_one, half_index * (S // 2), S // 2, 3)
    entries_half = join_halves(entries_two, peer_two, quarter_index % 2)
    update_far, entries_far = swapped((update_one, entries_half), "leaf", 1)
    map_near = lax.dynamic_index_in_dim(map_two, pair_index, 0, keepdims=False)
    map_far = lax.dynamic_index_in_dim(map_two, jnp.bitwise_xor(pair_index, 1), 0, keepdims=False)
    near_rows = update_one.reshape(batch_count, local_tiles, TILE, U)
    far_rows = update_far.reshape(batch_count, local_tiles, TILE, U)
    front_second = place_child(near_rows, map_near, column) + place_child(far_rows, map_far, column)
    initial_two = join_halves(entries_half, entries_far, side_index)
    mask_second = lax.dynamic_index_in_dim(mask_two, quad_index, 0, keepdims=False)
    front_second = add_initial(front_second, initial_two, mask_second, column)
    factor_rows_two, update_last = factor_front(front_second, column)
    update_last = lax.dynamic_slice_in_dim(update_last, quarter_index * (U // 4), U // 4, 2)
    factor_two = lax.dynamic_slice_in_dim(factor_rows_two, quarter_index * (S // 4), S // 4, 3)
    update_two = update_last.reshape(batch_count, local_tiles, TILE, U // 4)
    return (factor_one[None, None], factor_two[None, None], update_two[None, None])


def solution(mesh):
    return jax.shard_map(
        body,
        mesh=mesh,
        in_specs=(
            P("leaf", "front", None, None, None, None),
            P("leaf", "front", None, None, None, None),
            P("leaf", "front", None, None, None, None),
            P(),
            P(),
            P(),
            P(),
        ),
        out_specs=(
            P("leaf", "front", None, None, None, None),
            P("leaf", "front", None, None, None, None),
            P("leaf", "front", None, None, None, None),
        ),
        check_vma=False,
    )
```

profile of v0, /device:TPU:1, one launch (start us, length us, event | category | flops | bytes accessed | tf_op | source)
XLA Modules:
  0.0 1299.8 jit_solution(7646188197757473696)
XLA Ops:
  74.5 13.8 %select_add_fusion.1 = f32[1,4,256,16,256]{4,2,1,3,0:T(8,128)} fusion(bf16[16,4,256,256]{3,2,1,0:T(8,128)(2,1)} %gather_fusion.3, bf16[16,4,256,256]{3,2,1,0:T(8,128)(2,1)} %gather_fusion.1, pred[16]{0:T(512)(128)(4,1)S(1)} %and_bitcast_fusion.4, pred[16]{0:T(512)(128)(4,1)S(1)} %and_bitcast_fusion.6, pred[4,16]{0,1:T(8,128)(4,1)S(1)} %broadcast_and_fusion.2, ...), kind=kLoop, calls=%fused_computation.13 | loop fusion | flops 29360128 | bytes 33554592 | tf_op jit(solution)/shard_map/add | solution.py:115
  88.3 16.4 %copy.145 = f32[1,4,256,16,256]{2,4,3,1,0:T(8,128)} copy(f32[1,4,256,16,256]{4,2,1,3,0:T(8,128)} %select_add_fusion.1) | data formatting | bytes 33554432 | tf_op jit(solution)/shard_map/add | solution.py:115
  116.7 47.7 %all-gather.11.cloned.1.call-done = f32[4,1,256,1024]{3,2,1,0:T(8,128)} async-done(((f32[1,1,256,1024]{3,2,1,0:T(8,128)}), f32[4,1,256,1024]{3,2,1,0:T(8,128)}) %all-gather.11.cloned.1.call-update) | async-done | bytes 4194320 | tf_op jit(solution)/shard_map/all_gather | solution.py:75
  176.6 11.7 custom-call.91
  205.2 11.9 custom-call.93
  231.5 11.7 custom-call.95
  257.9 11.9 custom-call.97
  284.4 11.7 custom-call.99
  297.5 10.2 custom-call.100
  311.0 11.7 custom-call.101
  336.8 11.9 custom-call.103
  362.3 11.7 custom-call.105
  387.9 28.1 %while.4 = (s32[]{:T(128)}, f32[1,1024,1024]{2,1,0:T(8,128)}, s32[8,2]{0,1:T(2,128)S(1)}, f32[8,1,128,128]{3,2,1,0:T(8,128)}, s32[]{:T(128)}) while((s32[]{:T(128)}, f32[1,1024,1024]{2,1,0:T(8,128)}, s32[8,2]{0,1:T(2,128)S(1)}, f32[8,1,128,128]{3,2,1,0:T(8,128)}, s32[]{:T(128)}) %tuple.131), condition=%wide.while_cond, body=%wide.while_body.sunk | while | flops 2 | bytes 132205 | solution.py:79
  416.0 80.4 %custom-call.106 = f32[1,8,128,128]{2,3,1,0:T(8,128)} custom-call(f32[1,8,128,128]{3,2,1,0:T(8,128)} %bitcast.928), custom_call_target="InvertDiagBlocksLowerTriangular" | custom-call | tf_op jit(solution)/shard_map/triangular_solve/custom-call.7 | solution.py:79
  549.6 50.9 %all-gather.7.cloned.1.call-done = bf16[4,1,3,256,1024]{4,3,2,1,0:T(8,128)(2,1)} async-done(((bf16[1,1,3,256,1024]{4,3,2,1,0:T(8,128)(2,1)}), bf16[4,1,3,256,1024]{4,3,2,1,0:T(8,128)(2,1)}) %all-gather.7.cloned.1.call-update) | async-done | bytes 6291472 | tf_op jit(solution)/shard_map/all_gather | solution.py:83
  654.7 61.9 %collective-permute-done.2 = bf16[1,768,3072]{2,1,0:T(8,128)(2,1)} collective-permute-done((bf16[1,768,3072]{2,1,0:T(8,128)(2,1)}, bf16[1,768,3072]{2,1,0:T(8,128)(2,1)}, u32[]{:S(2)}, u32[]{:S(2)}) %collective-permute-start.2) | collective-permute-done | bytes 4718624 | tf_op jit(solution)/shard_map/ppermute | solution.py:18
  752.2 13.8 %select_add_fusion = f32[1,4,256,16,256]{4,2,1,3,0:T(8,128)} fusion(bf16[16,4,256,256]{3,2,1,0:T(8,128)(2,1)} %gather_fusion.7, bf16[16,4,256,256]{3,2,1,0:T(8,128)(2,1)} %gather_fusion.5, pred[16]{0:T(512)(128)(4,1)S(1)} %and_bitcast_fusion, pred[16]{0:T(512)(128)(4,1)S(1)} %and_bitcast_fusion.2, pred[4,16]{0,1:T(8,128)(4,1)S(1)} %broadcast_and_fusion, ...), kind=kLoop, calls=%fused_computation.12 | loop fusion | flops 29360128 | bytes 33554592 | tf_op jit(solution)/shard_map/add | solution.py:129
  766.0 16.4 %copy.163 = f32[1,4,256,16,256]{2,4,3,1,0:T(8,128)} copy(f32[1,4,256,16,256]{4,2,1,3,0:T(8,128)} %select_add_fusion) | data formatting | bytes 33554432 | tf_op jit(solution)/shard_map/add | solution.py:129
  793.6 49.4 %all-gather.13.cloned.1.call-done = f32[4,1,256,1024]{3,2,1,0:T(8,128)} async-done(((f32[1,1,256,1024]{3,2,1,0:T(8,128)}), f32[4,1,256,1024]{3,2,1,0:T(8,128)}) %all-gather.13.cloned.1.call-update) | async-done | bytes 4194320 | tf_op jit(solution)/shard_map/all_gather | solution.py:75
  854.9 11.7 custom-call.111
  883.5 11.9 custom-call.113
  909.9 11.7 custom-call.115
  936.2 12.1 custom-call.117
  962.9 11.7 custom-call.119
  975.9 9.9 custom-call.120
  989.2 11.7 custom-call.121
  1015.0 11.9 custom-call.123
  1040.6 11.7 custom-call.125
  1066.2 28.1 %while.5 = (s32[]{:T(128)}, f32[1,1024,1024]{2,1,0:T(8,128)}, s32[8,2]{0,1:T(2,128)S(1)}, f32[8,1,128,128]{3,2,1,0:T(8,128)}, s32[]{:T(128)}) while((s32[]{:T(128)}, f32[1,1024,1024]{2,1,0:T(8,128)}, s32[8,2]{0,1:T(2,128)S(1)}, f32[8,1,128,128]{3,2,1,0:T(8,128)}, s32[]{:T(128)}) %tuple.145), condition=%wide.while_cond.clone, body=%wide.while_body.clone.sunk | while | flops 2 | bytes 132205 | solution.py:79
  1094.3 80.4 %custom-call.126 = f32[1,8,128,128]{2,3,1,0:T(8,128)} custom-call(f32[1,8,128,128]{3,2,1,0:T(8,128)} %bitcast.927), custom_call_target="InvertDiagBlocksLowerTriangular" | custom-call | tf_op jit(solution)/shard_map/triangular_solve/custom-call.7 | solution.py:79
  1227.9 10.1 copy.173
  1244.0 37.3 %all-gather.9.cloned.1.call-done = bf16[4,1,3,256,1024]{4,3,2,1,0:T(8,128)(2,1)} async-done(((bf16[1,1,3,256,1024]{4,3,2,1,0:T(8,128)(2,1)}), bf16[4,1,3,256,1024]{4,3,2,1,0:T(8,128)(2,1)}) %all-gather.9.cloned.1.call-update) | async-done | bytes 6291472 | tf_op jit(solution)/shard_map/all_gather | solution.py:83
  (354 shorter events, 587.5 us)
Async XLA Ops:
  7.2 11.9 copy-start
  7.2 157.2 %all-gather.11.cloned.1.call-start = ((), (), s32[]{:S(2)}) async-start(), calls=%async_computation.2 | async-start | bytes 5242880 | tf_op jit(solution)/shard_map/all_gather | solution.py:75
  8.7 10.0 copy-start.18
  8.7 10.8 copy-start.19
  8.7 11.2 copy-start.17
  8.7 95.9 %collective-permute-start.1 = (bf16[1,4,256,512]{2,3,1,0:T(8,128)(2,1)S(1)}, bf16[1,4,256,512]{2,3,1,0:T(8,128)(2,1)S(1)}, u32[]{:S(2)}, u32[]{:S(2)}) collective-permute-start(bf16[1,4,256,512]{2,3,1,0:T(8,128)(2,1)S(1)} %bitcast.921), channel_id=1, source_target_pairs={{0,4},{4,0},{8,12},{12,8},{16,20},{20,16},{24,28},{28,24},{32,36},... | collective-permute-start | bytes 3145736 | tf_op jit(solution)/shard_map/ppermute | solution.py:18
  18.7 29.6 %collective-permute-start = (bf16[1,3,256,3072]{2,3,1,0:T(8,128)(2,1)}, bf16[1,3,256,3072]{2,3,1,0:T(8,128)(2,1)}, u32[]{:S(2)}, u32[]{:S(2)}) collective-permute-start(bf16[1,3,256,3072]{2,3,1,0:T(8,128)(2,1)} %bitcast.880), channel_id=1, source_target_pairs={{0,4},{4,0},{8,12},{12,8},{16,20},{20,16},{24,28},{28,24},{32,36},... | collective-permute-start | bytes 14155784 | tf_op jit(solution)/shard_map/ppermute | solution.py:18
  109.0 2.0 copy-start.2
  112.3 1.9 slice-start
  112.4 488.2 %all-gather.7.cloned.1.call-start = ((), (), s32[]{:S(2)}) async-start(), calls=%async_computation | async-start | bytes 7864320 | tf_op jit(solution)/shard_map/all_gather | solution.py:83
  174.6 1.9 copy-start.10
  380.3 116.2 %copy-start.9 = (f32[1,3,256,1024]{3,2,1,0:T(8,128)S(1)}, f32[1,3,256,1024]{3,2,1,0:T(8,128)}, u32[]{:S(2)}) copy-start(f32[1,3,256,1024]{3,2,1,0:T(8,128)} %copy.152) | copy-start | bytes 9437188
  496.4 6.9 copy-start.14
  528.4 1.7 copy-start.4
  531.8 311.2 %all-gather.13.cloned.1.call-start = ((), (), s32[]{:S(2)}) async-start(), calls=%async_computation.3 | async-start | bytes 5242880 | tf_op jit(solution)/shard_map/all_gather | solution.py:75
  600.5 5.5 copy-start.12
  606.0 8.9 copy-start.16
  613.7 102.9 %collective-permute-start.2 = (bf16[1,768,3072]{2,1,0:T(8,128)(2,1)}, bf16[1,768,3072]{2,1,0:T(8,128)(2,1)}, u32[]{:S(2)}, u32[]{:S(2)}) collective-permute-start(bf16[1,768,3072]{2,1,0:T(8,128)(2,1)} %bitcast.920), channel_id=1, source_target_pairs={{0,8},{4,12},{8,0},{12,4},{16,24},{20,28},{24,16},{28,20},{32,40},... | collective-permute-start | bytes 14155784 | tf_op jit(solution)/shard_map/ppermute | solution.py:18
  615.2 2.6 collective-permute-start.3
  618.0 164.3 %collective-permute-start.4 = (bf16[1,4,256,512]{2,3,1,0:T(8,128)(2,1)S(1)}, bf16[1,4,256,512]{2,3,1,0:T(8,128)(2,1)}, u32[]{:S(2)}, u32[]{:S(2)}) collective-permute-start(bf16[1,4,256,512]{2,3,1,0:T(8,128)(2,1)S(1)} %maximum_select_fusion.3), channel_id=1, source_target_pairs={{0,8},{4,12},{8,0},{12,4},{16,24},{20,28},{24,16},{28,20},{32,40},... | collective-permute-start | bytes 3145736 | tf_op jit(solution)/shard_map/ppermute | solution.py:18
  785.9 2.0 copy-start.3
  789.3 1.9 slice-start.1
  789.3 492.0 %all-gather.9.cloned.1.call-start = ((), (), s32[]{:S(2)}) async-start(), calls=%async_computation.1 | async-start | bytes 7864320 | tf_op jit(solution)/shard_map/all_gather | solution.py:83
  853.0 1.9 copy-start.11
  1058.6 116.1 %copy-start.8 = (f32[1,3,256,1024]{3,2,1,0:T(8,128)S(1)}, f32[1,3,256,1024]{3,2,1,0:T(8,128)}, u32[]{:S(2)}) copy-start(f32[1,3,256,1024]{3,2,1,0:T(8,128)} %copy.171) | copy-start | bytes 9437188
  1174.7 6.9 copy-start.15
  1206.7 1.7 copy-start.6
  1208.4 4.1 copy-start.5
  1227.9 10.1 copy-start.7
  1244.0 40.8 %copy-start.13 = (bf16[1,768,1024]{1,2,0:T(8,128)(2,1)S(1)}, bf16[1,768,1024]{1,2,0:T(8,128)(2,1)}, u32[]{:S(2)}) copy-start(bf16[1,768,1024]{1,2,0:T(8,128)(2,1)} %convert_element_type.105) | copy-start | bytes 4718596
  1284.8 8.2 copy-start.1
Sparse Core Ops, SparseCore 0:
  112.5 51.8 all-gather.10
  532.0 68.5 all-gather.6
  789.4 53.5 all-gather.12
  1212.7 68.5 all-gather.8
where the time goes:
time: 1310 us; the launch traced here: 1300 us
  other arithmetic  602 us (46%)
  local copies, waits for them, and re-layouts  297 us (23%)
  waiting for transfers between devices  248 us (19%)
  matrix products  123 us (9%)
  between operations  25 us (2%)
    another operation x62, other arithmetic, factor_front(): lower_factor = jnp.linalg.cholesky(pivot_block)  346 us
    another operation x5, other arithmetic, factor_front(): lax.linalg.triangular_solve(lower_factor, coupling, left_side=False, lowe...  174 us
    all_gather x2, waiting for transfers between devices, factor_front(): pivot_all = lax.all_gather(pivot_piece[None], 'front', axis=0, tiled=True)  97.1 us
    all_gather x2, waiting for transfers between devices, factor_front(): lax.all_gather(panel_round.reshape(batch_count, local_tiles, TILE, S)[Non...  88.2 us
    another operation x30, matrix products, factor_front(): lax.linalg.triangular_solve(lower_factor, coupling, left_side=False, lowe...  63.6 us
    another operation x53, local copies, waits for them, and re-layouts, factor_front(): lax.linalg.triangular_solve(lower_factor, coupling, left_side=False, lowe...  62.7 us
    ppermute x5, waiting for transfers between devices, swapped(): return lax.ppermute(value, axis, pairs)  62.4 us
    another operation x28, matrix products, factor_front(): lower_factor = jnp.linalg.cholesky(pivot_block)  46.3 us
  transfers between devices with their start and end apart: 9, of which 6 were waited for; matrix products, arithmetic and copies ran while one was open for 19% of the time, Pallas kernels for 0%

commit v1 on v0

--- a/solution.py
+++ b/solution.py
@@ -72,7 +72,10 @@
     local_tiles = canvas.shape[1] - 1
     groups = lax.axis_size("front")
     pivot_piece = canvas[:, :1, :, :S]
-    pivot_all = lax.all_gather(pivot_piece[None], "front", axis=0, tiled=True)
+    pivot_all = jnp.concatenate(
+        lax.all_to_all(jnp.stack([pivot_piece[None]] * lax.axis_size("front")), "front", 0, 0),
+        axis=0,
+    )
     pivot_block = jnp.moveaxis(pivot_all, 0, 2).reshape(batch_count, S, S)
     lower_factor = jnp.linalg.cholesky(pivot_block)
     coupling = canvas[:, 1:, :, :S].reshape(batch_count, local_tiles * TILE, S)

time: 1310 us -> 1340 us (1.023)
  local copies, waits for them, and re-layouts: 297 us -> 323 us
    all_gather x2 -> x0, waiting for transfers between devices: 97.1 us -> none  [factor_front(): pivot_all = lax.all_gather(pivot_piece[None], 'front', axis=0, tiled=True)]
    all_to_all x0 -> x2, waiting for transfers between devices: none -> 85.5 us  [factor_front(): lax.all_to_all(jnp.stack([pivot_piece[None]] * lax.axis_size('front')), '...]
    all_to_all x0 -> x2, local copies, waits for them, and re-layouts: none -> 13.7 us  [factor_front(): lax.all_to_all(jnp.stack([pivot_piece[None]] * lax.axis_size('front')), '...]
where the time goes in v1:
time: 1340 us; the launch traced here: 1330 us
  other arithmetic  601 us (45%)
  local copies, waits for them, and re-layouts  323 us (24%)
  waiting for transfers between devices  238 us (18%)
  matrix products  123 us (9%)
  between operations  25.5 us (2%)
  starting transfers between devices  16.3 us (1%)
    another operation x62, other arithmetic, factor_front(): lower_factor = jnp.linalg.cholesky(pivot_block)  346 us
    another operation x5, other arithmetic, factor_front(): lax.linalg.triangular_solve(lower_factor, coupling, left_side=False, lowe...  174 us
    all_gather x2, waiting for transfers between devices, factor_front(): lax.all_gather(panel_round.reshape(batch_count, local_tiles, TILE, S)[Non...  90.1 us
    all_to_all x2, waiting for transfers between devices, factor_front(): lax.all_to_all(jnp.stack([pivot_piece[None]] * lax.axis_size('front')), '...  85.5 us
    another operation x30, matrix products, factor_front(): lax.linalg.triangular_solve(lower_factor, coupling, left_side=False, lowe...  64.1 us
    ppermute x5, waiting for transfers between devices, swapped(): return lax.ppermute(value, axis, pairs)  62.8 us
    another operation x53, local copies, waits for them, and re-layouts, factor_front(): lax.linalg.triangular_solve(lower_factor, coupling, left_side=False, lowe...  62.7 us
    another operation x28, matrix products, factor_front(): lower_factor = jnp.linalg.cholesky(pivot_block)  46.3 us
  transfers between devices with their start and end apart: 9, of which 6 were waited for; matrix products, arithmetic and copies ran while one was open for 19% of the time, Pallas kernels for 0%

profile of v1, /device:TPU:1, one launch (start us, length us, event | category | flops | bytes accessed | tf_op | source)
XLA Modules:
  0.0 1327.4 jit_solution(13973304165547474013)
XLA Ops:
  74.5 13.8 %select_add_fusion.1 = f32[1,4,256,16,256]{4,2,1,3,0:T(8,128)} fusion(bf16[16,4,256,256]{3,2,1,0:T(8,128)(2,1)} %gather_fusion.3, bf16[16,4,256,256]{3,2,1,0:T(8,128)(2,1)} %gather_fusion.1, pred[16]{0:T(512)(128)(4,1)S(1)} %and_bitcast_fusion.4, pred[16]{0:T(512)(128)(4,1)S(1)} %and_bitcast_fusion.6, pred[4,16]{0,1:T(8,128)(4,1)S(1)} %broadcast_and_fusion.2, ...), kind=kLoop, calls=%fused_computation.13 | loop fusion | flops 29360128 | bytes 33554592 | tf_op jit(solution)/shard_map/add | solution.py:118
  88.2 16.4 %copy.139 = f32[1,4,256,16,256]{2,4,3,1,0:T(8,128)} copy(f32[1,4,256,16,256]{4,2,1,3,0:T(8,128)} %select_add_fusion.1) | data formatting | bytes 33554432 | tf_op jit(solution)/shard_map/add | solution.py:118
  122.5 44.1 %all-to-all-done = f32[4,1,1,1,256,1024]{4,5,3,2,1,0:T(8,128)} async-done(((f32[4,1,1,1,256,1024]{4,5,3,2,1,0:T(8,128)}), f32[4,1,1,1,256,1024]{4,5,3,2,1,0:T(8,128)}, u32[]{:S(2)}, u32[]{:S(2)}) %all-to-all-start) | async-done | bytes 4194336 | tf_op jit(solution)/shard_map/all_to_all | solution.py:76
  191.0 11.7 custom-call.91
  219.6 11.9 custom-call.93
  245.9 11.7 custom-call.95
  272.3 11.9 custom-call.97
  298.9 11.7 custom-call.99
  311.9 10.2 custom-call.100
  325.4 11.7 custom-call.101
  351.2 11.9 custom-call.103
  376.9 11.7 custom-call.105
  402.5 28.1 %while.4 = (s32[]{:T(128)}, f32[1,1024,1024]{2,1,0:T(8,128)}, s32[8,2]{0,1:T(2,128)S(1)}, f32[8,1,128,128]{3,2,1,0:T(8,128)}, s32[]{:T(128)}) while((s32[]{:T(128)}, f32[1,1024,1024]{2,1,0:T(8,128)}, s32[8,2]{0,1:T(2,128)S(1)}, f32[8,1,128,128]{3,2,1,0:T(8,128)}, s32[]{:T(128)}) %tuple.131), condition=%wide.while_cond, body=%wide.while_body.sunk | while | flops 2 | bytes 132205 | solution.py:82
  430.6 80.2 %custom-call.106 = f32[1,8,128,128]{2,3,1,0:T(8,128)} custom-call(f32[1,8,128,128]{3,2,1,0:T(8,128)} %bitcast.930), custom_call_target="InvertDiagBlocksLowerTriangular" | custom-call | tf_op jit(solution)/shard_map/triangular_solve/custom-call.7 | solution.py:82
  564.4 50.3 %all-gather.3.cloned.1.call-done = bf16[4,1,3,256,1024]{4,3,2,1,0:T(8,128)(2,1)} async-done(((bf16[1,1,3,256,1024]{4,3,2,1,0:T(8,128)(2,1)}), bf16[4,1,3,256,1024]{4,3,2,1,0:T(8,128)(2,1)}) %all-gather.3.cloned.1.call-update) | async-done | bytes 6291472 | tf_op jit(solution)/shard_map/all_gather | solution.py:86
  668.5 62.3 %collective-permute-done.2 = bf16[1,768,3072]{2,1,0:T(8,128)(2,1)} collective-permute-done((bf16[1,768,3072]{2,1,0:T(8,128)(2,1)}, bf16[1,768,3072]{2,1,0:T(8,128)(2,1)}, u32[]{:S(2)}, u32[]{:S(2)}) %collective-permute-start.2) | collective-permute-done | bytes 4718624 | tf_op jit(solution)/shard_map/ppermute | solution.py:18
  766.4 13.8 %select_add_fusion = f32[1,4,256,16,256]{4,2,1,3,0:T(8,128)} fusion(bf16[16,4,256,256]{3,2,1,0:T(8,128)(2,1)} %gather_fusion.7, bf16[16,4,256,256]{3,2,1,0:T(8,128)(2,1)} %gather_fusion.5, pred[16]{0:T(512)(128)(4,1)S(1)} %and_bitcast_fusion, pred[16]{0:T(512)(128)(4,1)S(1)} %and_bitcast_fusion.2, pred[4,16]{0,1:T(8,128)(4,1)S(1)} %broadcast_and_fusion, ...), kind=kLoop, calls=%fused_computation.12 | loop fusion | flops 29360128 | bytes 33554592 | tf_op jit(solution)/shard_map/add | solution.py:132
  780.2 16.4 %copy.156 = f32[1,4,256,16,256]{2,4,3,1,0:T(8,128)} copy(f32[1,4,256,16,256]{4,2,1,3,0:T(8,128)} %select_add_fusion) | data formatting | bytes 33554432 | tf_op jit(solution)/shard_map/add | solution.py:132
  814.1 41.4 %all-to-all-done.1 = f32[4,1,1,1,256,1024]{4,5,3,2,1,0:T(8,128)} async-done(((f32[4,1,1,1,256,1024]{4,5,3,2,1,0:T(8,128)}), f32[4,1,1,1,256,1024]{4,5,3,2,1,0:T(8,128)}, u32[]{:S(2)}, u32[]{:S(2)}) %all-to-all-start.1) | async-done | bytes 4194336 | tf_op jit(solution)/shard_map/all_to_all | solution.py:76
  879.8 11.7 custom-call.111
  908.4 11.9 custom-call.113
  934.7 11.7 custom-call.115
  961.1 11.9 custom-call.117
  987.7 11.7 custom-call.119
  1000.7 10.2 custom-call.120
  1014.2 11.7 custom-call.121
  1040.0 11.9 custom-call.123
  1065.7 11.7 custom-call.125
  1091.3 28.1 %while.5 = (s32[]{:T(128)}, f32[1,1024,1024]{2,1,0:T(8,128)}, s32[8,2]{0,1:T(2,128)S(1)}, f32[8,1,128,128]{3,2,1,0:T(8,128)}, s32[]{:T(128)}) while((s32[]{:T(128)}, f32[1,1024,1024]{2,1,0:T(8,128)}, s32[8,2]{0,1:T(2,128)S(1)}, f32[8,1,128,128]{3,2,1,0:T(8,128)}, s32[]{:T(128)}) %tuple.141), condition=%wide.while_cond.clone, body=%wide.while_body.clone.sunk | while | flops 2 | bytes 132205 | solution.py:82
  1119.4 80.2 %custom-call.126 = f32[1,8,128,128]{2,3,1,0:T(8,128)} custom-call(f32[1,8,128,128]{3,2,1,0:T(8,128)} %bitcast.929), custom_call_target="InvertDiagBlocksLowerTriangular" | custom-call | tf_op jit(solution)/shard_map/triangular_solve/custom-call.7 | solution.py:82
  1252.4 10.4 copy.165
  1268.8 39.8 %all-gather.5.cloned.1.call-done = bf16[4,1,3,256,1024]{4,3,2,1,0:T(8,128)(2,1)} async-done(((bf16[1,1,3,256,1024]{4,3,2,1,0:T(8,128)(2,1)}), bf16[4,1,3,256,1024]{4,3,2,1,0:T(8,128)(2,1)}) %all-gather.5.cloned.1.call-update) | async-done | bytes 6291472 | tf_op jit(solution)/shard_map/all_gather | solution.py:86
  (356 shorter events, 624.1 us)
Async XLA Ops:
  7.2 11.9 copy-start
  8.7 10.0 copy-start.18
  8.7 10.8 copy-start.19
  8.7 11.2 copy-start.17
  8.7 95.9 %collective-permute-start.1 = (bf16[1,4,256,512]{2,3,1,0:T(8,128)(2,1)S(1)}, bf16[1,4,256,512]{2,3,1,0:T(8,128)(2,1)S(1)}, u32[]{:S(2)}, u32[]{:S(2)}) collective-permute-start(bf16[1,4,256,512]{2,3,1,0:T(8,128)(2,1)S(1)} %bitcast.923), channel_id=1, source_target_pairs={{0,4},{4,0},{8,12},{12,8},{16,20},{20,16},{24,28},{28,24},{32,36},... | collective-permute-start | bytes 3145736 | tf_op jit(solution)/shard_map/ppermute | solution.py:18
  18.7 29.6 %collective-permute-start = (bf16[1,3,256,3072]{2,3,1,0:T(8,128)(2,1)}, bf16[1,3,256,3072]{2,3,1,0:T(8,128)(2,1)}, u32[]{:S(2)}, u32[]{:S(2)}) collective-permute-start(bf16[1,3,256,3072]{2,3,1,0:T(8,128)(2,1)} %bitcast.886), channel_id=1, source_target_pairs={{0,4},{4,0},{8,12},{12,8},{16,20},{20,16},{24,28},{28,24},{32,36},... | collective-permute-start | bytes 14155784 | tf_op jit(solution)/shard_map/ppermute | solution.py:18
  108.9 2.0 copy-start.2
  113.3 53.4 %all-to-all-start = ((f32[4,1,1,1,256,1024]{4,5,3,2,1,0:T(8,128)}), f32[4,1,1,1,256,1024]{4,5,3,2,1,0:T(8,128)}, u32[]{:S(2)}, u32[]{:S(2)}) async-start(f32[4,1,1,1,256,1024]{4,5,3,2,1,0:T(8,128)} %stack.6), calls=%async_computation | async-start | bytes 8388608 | tf_op jit(solution)/shard_map/all_to_all | solution.py:76
  118.2 1.9 slice-start
  118.2 496.6 %all-gather.3.cloned.1.call-start = ((), (), s32[]{:S(2)}) async-start(), calls=%async_computation.2 | async-start | bytes 7864320 | tf_op jit(solution)/shard_map/all_gather | solution.py:86
  189.1 1.9 copy-start.10
  394.9 116.0 %copy-start.9 = (f32[1,3,256,1024]{3,2,1,0:T(8,128)S(1)}, f32[1,3,256,1024]{3,2,1,0:T(8,128)}, u32[]{:S(2)}) copy-start(f32[1,3,256,1024]{3,2,1,0:T(8,128)} %copy.145) | copy-start | bytes 9437188
  510.8 6.9 copy-start.14
  543.0 1.7 copy-start.4
  614.8 5.5 copy-start.12
  620.3 8.9 copy-start.16
  627.9 102.9 %collective-permute-start.2 = (bf16[1,768,3072]{2,1,0:T(8,128)(2,1)}, bf16[1,768,3072]{2,1,0:T(8,128)(2,1)}, u32[]{:S(2)}, u32[]{:S(2)}) collective-permute-start(bf16[1,768,3072]{2,1,0:T(8,128)(2,1)} %bitcast.922), channel_id=1, source_target_pairs={{0,8},{4,12},{8,0},{12,4},{16,24},{20,28},{24,16},{28,20},{32,40},... | collective-permute-start | bytes 14155784 | tf_op jit(solution)/shard_map/ppermute | solution.py:18
  629.4 2.6 collective-permute-start.3
  632.3 164.3 %collective-permute-start.4 = (bf16[1,4,256,512]{2,3,1,0:T(8,128)(2,1)S(1)}, bf16[1,4,256,512]{2,3,1,0:T(8,128)(2,1)}, u32[]{:S(2)}, u32[]{:S(2)}) collective-permute-start(bf16[1,4,256,512]{2,3,1,0:T(8,128)(2,1)S(1)} %maximum_select_fusion.3), channel_id=1, source_target_pairs={{0,8},{4,12},{8,0},{12,4},{16,24},{20,28},{24,16},{28,20},{32,40},... | collective-permute-start | bytes 3145736 | tf_op jit(solution)/shard_map/ppermute | solution.py:18
  800.1 2.0 copy-start.3
  804.5 51.0 %all-to-all-start.1 = ((f32[4,1,1,1,256,1024]{4,5,3,2,1,0:T(8,128)}), f32[4,1,1,1,256,1024]{4,5,3,2,1,0:T(8,128)}, u32[]{:S(2)}, u32[]{:S(2)}) async-start(f32[4,1,1,1,256,1024]{4,5,3,2,1,0:T(8,128)} %stack.7), calls=%async_computation.1 | async-start | bytes 8388608 | tf_op jit(solution)/shard_map/all_to_all | solution.py:76
  809.4 1.9 slice-start.1
  809.4 499.2 %all-gather.5.cloned.1.call-start = ((), (), s32[]{:S(2)}) async-start(), calls=%async_computation.3 | async-start | bytes 7864320 | tf_op jit(solution)/shard_map/all_gather | solution.py:86
  877.9 1.9 copy-start.11
  1083.7 116.0 %copy-start.8 = (f32[1,3,256,1024]{3,2,1,0:T(8,128)S(1)}, f32[1,3,256,1024]{3,2,1,0:T(8,128)}, u32[]{:S(2)}) copy-start(f32[1,3,256,1024]{3,2,1,0:T(8,128)} %copy.163) | copy-start | bytes 9437188
  1199.6 6.9 copy-start.15
  1231.8 1.7 copy-start.6
  1233.5 4.1 copy-start.5
  1252.4 10.4 copy-start.7
  1268.8 43.3 %copy-start.13 = (bf16[1,768,1024]{1,2,0:T(8,128)(2,1)S(1)}, bf16[1,768,1024]{1,2,0:T(8,128)(2,1)}, u32[]{:S(2)}) copy-start(bf16[1,768,1024]{1,2,0:T(8,128)(2,1)} %convert_element_type.105) | copy-start | bytes 4718596
  1312.1 8.2 copy-start.1
Sparse Core Ops, SparseCore 0:
  546.6 68.0 all-gather.2
  1237.8 70.7 all-gather.4
